TPU v7x, 32 devices: a whole 2x2x4 slice. The times are simulated.
32 devices in a mesh: member: 2 (over y), vec: 4 (over x, core), band: 4 (over z).
Axes of the slice: x: 2, y: 2, z: 4, core: 2. Of those that a mesh axis runs over, the one named last changes fastest.
Arguments:
- vectors: float32 [32, 3, 16, 1440], P(('member', 'vec'), None, 'band'), parts along dimension 0, may hold values from -6 to 6
- flow: float32 [4, 16, 1440], P(None, 'band'), may hold values from -1 to 1
- band_cut: int32 [16], replicated, may hold values from 2 to 127
- order: int32 [4], replicated, may hold values from 0 to 3, each once
Outputs:
- basis: float32 [32, 3, 16, 1440], P(('member', 'vec'), None, 'band'), parts along dimension 0
- growth: float32 [32], P(('member', 'vec')), parts along dimension 0
There are 2 independent parts, one for each index of `member`. A program takes and returns all parts, laid end to end along the dimension named above; an argument that names none is the same for every part. Nothing has to cross between parts.
Inputs may be any that keep to these rules, and one draw needn't show every extreme that they name: `order`: each block number appears once.
All inputs are finite; a program needn't handle non-finite values.
Results may differ from a plain program's by a relative error of at most 0.0001.
Values sent between devices are 32-bit elements; how exact they have to be, the bound alone decides.
A program may use at most 64 MiB of HBM per device.

v0:
```python
import math

import jax
import jax.numpy as jnp
from jax import lax
from jax.sharding import PartitionSpec as P

KMAX = 128
CAP_DEV = 2


step_dt = 0.4
half_dt = 0.2
sixth_dt = 0.4 / 6.0


def extended(block, sides, width):
    for axis, dim in sides:
        count = lax.axis_size(axis)
        forward = [(i, i + 1) for i in range(count - 1)]
        backward = [(target, source) for source, target in forward]
        low = lax.ppermute(
            lax.slice_in_dim(block, block.shape[dim] - width, None, axis=dim), axis, forward
        )
        high = lax.ppermute(lax.slice_in_dim(block, 0, width, axis=dim), axis, backward)
        block = jnp.concatenate([low, block, high], axis=dim)
    return block


def broadcast(value, axis, source):
    kept = jnp.where(lax.axis_index(axis) == source, value, 0).astype(value.dtype)
    return lax.psum(kept, axis)


def tendency(z, coef):
    inner = z[:, :, 1:-1]
    dx = 0.5 * (jnp.roll(inner, -1, 3) - jnp.roll(inner, 1, 3))
    dy = 0.5 * (z[:, :, 2:] - z[:, :, :-2])
    speed_x = coef[0]
    speed_y = coef[1]
    depth = 1.0 + 0.5 * coef[2]
    rotation = 0.5 * coef[3]
    advect = -(speed_x * dx + speed_y * dy)
    t_height = advect[:, 0] - depth * (dx[:, 1] + dy[:, 2])
    t_zonal = advect[:, 1] - dx[:, 0] + rotation * inner[:, 2]
    t_merid = advect[:, 2] - dy[:, 0] - rotation * inner[:, 1]
    return jnp.stack([t_height, t_zonal, t_merid], 1)


def with_rows(state):
    return extended(state, (("band", 2),), 1)


def step_near(state, flow):
    k_one = tendency(with_rows(state), flow)
    k_two = tendency(with_rows(state + half_dt * k_one), flow)
    k_three = tendency(with_rows(state + half_dt * k_two), flow)
    k_four = tendency(with_rows(state + step_dt * k_three), flow)
    return state + sixth_dt * (k_one + 2.0 * k_two + 2.0 * k_three + k_four)


def mode_table(nlon, kmax):
    points = jnp.arange(nlon, dtype=jnp.int32)
    waves = jnp.arange(kmax, dtype=jnp.int32)
    phase = (waves[:, None] * points[None, :] % nlon).astype(jnp.float32) * (2.0 * math.pi / nlon)
    scale = jnp.where(waves == 0, math.sqrt(1.0 / nlon), math.sqrt(2.0 / nlon)).astype(jnp.float32)
    cosines = jnp.cos(phase) * scale[:, None]
    sines = jnp.sin(phase) * math.sqrt(2.0 / nlon)
    return jnp.concatenate([cosines, sines], 0)


def project(rows, cutoff, table, kmax):
    waves = jnp.arange(kmax, dtype=jnp.int32)
    wave_both = jnp.concatenate([waves, waves], 0)
    keep = (wave_both <= cutoff[..., None]).astype(jnp.float32)
    coeffs = jnp.einsum("...l,kl->...k", rows, table, precision=lax.Precision.HIGHEST)
    return jnp.einsum("...k,kl->...l", coeffs * keep, table, precision=lax.Precision.HIGHEST)


def polar_filter(state, band_cut, table):
    nband = lax.axis_size("band")
    me_band = lax.axis_index("band")
    lat_dev = state.shape[2]
    cap_rows = CAP_DEV * lat_dev
    north = me_band < CAP_DEV
    south = me_band >= nband - CAP_DEV
    start = jnp.where(north, me_band * lat_dev, cap_rows + (me_band - nband + CAP_DEV) * lat_dev)
    start = jnp.clip(start, 0, 2 * cap_rows - lat_dev)
    cutoff = lax.dynamic_slice_in_dim(band_cut, start, lat_dev)
    return lax.cond(
        north | south, lambda value: project(value, cutoff, table, KMAX), lambda value: value, state
    )


def on_device(vectors, flow, band_cut, order):
    state = vectors
    nband = lax.axis_size("band")
    lat_dev = state.shape[2]
    table = mode_table(state.shape[3], KMAX)
    for inner_step in range(2):
        state = step_near(state, flow)
    state = polar_filter(state, band_cut, table)
    nblocks = lax.axis_size("vec")
    me_vec = lax.axis_index("vec")
    vec_dev = state.shape[0]
    total = float(3 * nband * lat_dev * state.shape[3])
    flat = state.reshape(vec_dev, -1)
    numbers = jnp.arange(nblocks, dtype=jnp.int32)
    position = jnp.sum(jnp.where(order == me_vec, numbers, 0))
    growth = jnp.zeros((vec_dev,), jnp.float32)
    for turn in range(nblocks):
        panel = broadcast(flat, "vec", order[turn])
        gram = lax.psum(jnp.dot(panel, panel.T, precision=lax.Precision.HIGHEST), "band") / total
        lower = jnp.linalg.cholesky(gram)
        ortho = jax.scipy.linalg.solve_triangular(lower, panel, lower=True)
        coef = lax.psum(jnp.dot(flat, ortho.T, precision=lax.Precision.HIGHEST), "band") / total
        update = flat - jnp.dot(coef, ortho, precision=lax.Precision.HIGHEST)
        flat = jnp.where(position > turn, update, jnp.where(position == turn, ortho, flat))
        growth = jnp.where(position == turn, jnp.log(jnp.diagonal(lower)), growth)
    return (flat.reshape(state.shape), growth)


def solution(mesh):
    in_specs = (P(("member", "vec"), None, "band", None), P(None, "band", None), P(), P())
    out_specs = (P(("member", "vec"), None, "band", None), P(("member", "vec")))
    return jax.shard_map(
        on_device, mesh=mesh, in_specs=in_specs, out_specs=out_specs, check_vma=False
    )
```

profile of v0, /device:TPU:0, one launch (start us, length us, event | category | flops | bytes accessed | tf_op | source)
XLA Modules:
  0.0 348.0 jit_solution(16133141258340314673)
XLA Ops:
  7.2 1.9 fusion.110
  9.1 1.3 collective-permute-start
  10.4 5.6 %collective-permute-start.1 = (f32[4,3,1,1440]{3,2,1,0:T(1,128)}, f32[4,3,1,1440]{3,2,1,0:T(1,128)S(1)}, u32[]{:S(2)}, u32[]{:S(2)}) collective-permute-start(f32[4,3,1,1440]{3,2,1,0:T(1,128)} %get-tuple-element.172), channel_id=1, source_target_pairs={{0,1},{1,2},{2,3},{4,5},{5,6},{6,7},{8,9},{9,10},{10,11},{12,13},{... | collective-permute-start | bytes 207368 | tf_op jit(solution)/shard_map/ppermute | solution.py:22
  16.0 2.0 fusion.108
  18.1 3.1 sine_multiply_fusion
  21.9 0.7 fusion.111
  23.9 1.6 broadcast_multiply_fusion.15
  26.0 1.3 collective-permute-start.2
  27.3 4.6 %collective-permute-start.3 = (f32[4,3,1,1440]{3,2,1,0:T(1,128)S(1)}, f32[4,3,1,1440]{3,2,1,0:T(1,128)S(1)}, u32[]{:S(2)}, u32[]{:S(2)}) collective-permute-start(f32[4,3,1,1440]{3,2,1,0:T(1,128)S(1)} %get-tuple-element.166), channel_id=1, source_target_pairs={{0,1},{1,2},{2,3},{4,5},{5,6},{6,7},{8,9},{9,10},{10,11},{12,13},{... | collective-permute-start | bytes 207368 | tf_op jit(solution)/shard_map/ppermute | solution.py:22
  32.3 1.6 collective-permute-done.3
  34.9 1.3 collective-permute-start.4
  36.2 4.9 %collective-permute-start.5 = (f32[4,3,1,1440]{3,2,1,0:T(1,128)S(1)}, f32[4,3,1,1440]{3,2,1,0:T(1,128)S(1)}, u32[]{:S(2)}, u32[]{:S(2)}) collective-permute-start(f32[4,3,1,1440]{3,2,1,0:T(1,128)S(1)} %get-tuple-element.160), channel_id=1, source_target_pairs={{0,1},{1,2},{2,3},{4,5},{5,6},{6,7},{8,9},{9,10},{10,11},{12,13},{... | collective-permute-start | bytes 207368 | tf_op jit(solution)/shard_map/ppermute | solution.py:22
  41.5 1.6 collective-permute-done.5
  44.2 1.3 collective-permute-start.6
  45.5 4.9 %collective-permute-start.7 = (f32[4,3,1,1440]{3,2,1,0:T(1,128)S(1)}, f32[4,3,1,1440]{3,2,1,0:T(1,128)S(1)}, u32[]{:S(2)}, u32[]{:S(2)}) collective-permute-start(f32[4,3,1,1440]{3,2,1,0:T(1,128)S(1)} %get-tuple-element.154), channel_id=1, source_target_pairs={{0,1},{1,2},{2,3},{4,5},{5,6},{6,7},{8,9},{9,10},{10,11},{12,13},{... | collective-permute-start | bytes 207368 | tf_op jit(solution)/shard_map/ppermute | solution.py:22
  50.8 1.6 collective-permute-done.7
  53.6 1.3 collective-permute-start.8
  54.9 4.9 %collective-permute-start.9 = (f32[4,3,1,1440]{3,2,1,0:T(1,128)S(1)}, f32[4,3,1,1440]{3,2,1,0:T(1,128)S(1)}, u32[]{:S(2)}, u32[]{:S(2)}) collective-permute-start(f32[4,3,1,1440]{3,2,1,0:T(1,128)S(1)} %get-tuple-element.148), channel_id=1, source_target_pairs={{0,1},{1,2},{2,3},{4,5},{5,6},{6,7},{8,9},{9,10},{10,11},{12,13},{... | collective-permute-start | bytes 207368 | tf_op jit(solution)/shard_map/ppermute | solution.py:22
  60.2 1.6 collective-permute-done.9
  63.1 1.3 collective-permute-start.10
  64.4 5.1 %collective-permute-start.11 = (f32[4,3,1,1440]{3,2,1,0:T(1,128)S(1)}, f32[4,3,1,1440]{3,2,1,0:T(1,128)S(1)}, u32[]{:S(2)}, u32[]{:S(2)}) collective-permute-start(f32[4,3,1,1440]{3,2,1,0:T(1,128)S(1)} %get-tuple-element.142), channel_id=1, source_target_pairs={{0,1},{1,2},{2,3},{4,5},{5,6},{6,7},{8,9},{9,10},{10,11},{12,13},{... | collective-permute-start | bytes 207368 | tf_op jit(solution)/shard_map/ppermute | solution.py:22
  69.7 1.6 collective-permute-done.11
  72.5 1.3 collective-permute-start.12
  73.8 4.9 %collective-permute-start.13 = (f32[4,3,1,1440]{3,2,1,0:T(1,128)S(1)}, f32[4,3,1,1440]{3,2,1,0:T(1,128)S(1)}, u32[]{:S(2)}, u32[]{:S(2)}) collective-permute-start(f32[4,3,1,1440]{3,2,1,0:T(1,128)S(1)} %get-tuple-element.136), channel_id=1, source_target_pairs={{0,1},{1,2},{2,3},{4,5},{5,6},{6,7},{8,9},{9,10},{10,11},{12,13},{... | collective-permute-start | bytes 207368 | tf_op jit(solution)/shard_map/ppermute | solution.py:22
  79.1 1.6 collective-permute-done.13
  82.0 1.3 collective-permute-start.14
  83.3 4.9 %collective-permute-start.15 = (f32[4,3,1,1440]{3,2,1,0:T(1,128)S(1)}, f32[4,3,1,1440]{3,2,1,0:T(1,128)S(1)}, u32[]{:S(2)}, u32[]{:S(2)}) collective-permute-start(f32[4,3,1,1440]{3,2,1,0:T(1,128)S(1)} %get-tuple-element.130), channel_id=1, source_target_pairs={{0,1},{1,2},{2,3},{4,5},{5,6},{6,7},{8,9},{9,10},{10,11},{12,13},{... | collective-permute-start | bytes 207368 | tf_op jit(solution)/shard_map/ppermute | solution.py:22
  88.6 1.6 collective-permute-done.15
  91.4 2.6 conditional.1
  91.6 1.0 fusion.4
  92.7 1.4 fusion
  94.4 0.8 broadcast_select_fusion.3
  95.3 0.7 fusion.81
  97.8 32.7 %all-reduce.5.cloned.1.call-done = f32[4,17280]{1,0:T(4,128)} async-done(((f32[4,17280]{1,0:T(4,128)}), f32[4,17280]{1,0:T(4,128)}) %all-reduce.5.cloned.1.call-update) | async-done | bytes 276496 | tf_op jit(solution)/shard_map/psum | solution.py:32
  130.6 2.3 fusion.112
  132.9 11.7 %psum.85 = f32[4,4]{0,1:T(4,128)S(1)} all-reduce(f32[4,4]{0,1:T(4,128)S(1)} %fusion.112), channel_id=1, replica_groups=mesh['member'=2,'vec'=4,'band'=4] {'band'}, use_global_device_ids=true, to_apply=%region_4.5 | all-reduce | flops 16 | bytes 128 | tf_op jit(solution)/shard_map/psum | solution.py:113
  145.7 0.6 select_bitcast_fusion.3
  146.7 1.7 fusion.66
  148.4 1.3 fusion.113
  149.7 8.4 %psum.86 = f32[4,4]{0,1:T(4,128)S(1)} all-reduce(f32[4,4]{0,1:T(4,128)S(1)} %fusion.113), channel_id=1, replica_groups=mesh['member'=2,'vec'=4,'band'=4] {'band'}, use_global_device_ids=true, to_apply=%region_7.10 | all-reduce | flops 16 | bytes 128 | tf_op jit(solution)/shard_map/psum | solution.py:116
  158.1 1.5 broadcast_select_fusion.2
  161.5 29.0 %all-reduce.7.cloned.1.call-done = f32[4,17280]{1,0:T(4,128)} async-done(((f32[4,17280]{1,0:T(4,128)}), f32[4,17280]{1,0:T(4,128)}) %all-reduce.7.cloned.1.call-update) | async-done | bytes 276496 | tf_op jit(solution)/shard_map/psum | solution.py:32
  190.6 2.3 fusion.114
  192.9 11.9 %psum.88 = f32[4,4]{0,1:T(4,128)S(1)} all-reduce(f32[4,4]{0,1:T(4,128)S(1)} %fusion.114), channel_id=1, replica_groups=mesh['member'=2,'vec'=4,'band'=4] {'band'}, use_global_device_ids=true, to_apply=%region_9.12 | all-reduce | flops 16 | bytes 128 | tf_op jit(solution)/shard_map/psum | solution.py:113
  206.0 0.6 select_bitcast_fusion.2
  207.0 1.7 fusion.64
  208.7 1.3 fusion.115
  210.0 8.4 %psum.89 = f32[4,4]{0,1:T(4,128)S(1)} all-reduce(f32[4,4]{0,1:T(4,128)S(1)} %fusion.115), channel_id=1, replica_groups=mesh['member'=2,'vec'=4,'band'=4] {'band'}, use_global_device_ids=true, to_apply=%region_10.13 | all-reduce | flops 16 | bytes 128 | tf_op jit(solution)/shard_map/psum | solution.py:116
  218.3 1.5 broadcast_select_fusion.1
  221.8 29.0 %all-reduce.9.cloned.1.call-done = f32[4,17280]{1,0:T(4,128)} async-done(((f32[4,17280]{1,0:T(4,128)}), f32[4,17280]{1,0:T(4,128)}) %all-reduce.9.cloned.1.call-update) | async-done | bytes 276496 | tf_op jit(solution)/shard_map/psum | solution.py:32
  250.8 2.3 fusion.116
  253.2 11.7 %psum.91 = f32[4,4]{0,1:T(4,128)S(1)} all-reduce(f32[4,4]{0,1:T(4,128)S(1)} %fusion.116), channel_id=1, replica_groups=mesh['member'=2,'vec'=4,'band'=4] {'band'}, use_global_device_ids=true, to_apply=%region_12.15 | all-reduce | flops 16 | bytes 128 | tf_op jit(solution)/shard_map/psum | solution.py:113
  267.0 1.7 fusion.62
  268.7 1.3 fusion.117
  270.0 8.4 %psum.92 = f32[4,4]{0,1:T(4,128)S(1)} all-reduce(f32[4,4]{0,1:T(4,128)S(1)} %fusion.117), channel_id=1, replica_groups=mesh['member'=2,'vec'=4,'band'=4] {'band'}, use_global_device_ids=true, to_apply=%region_13.16 | all-reduce | flops 16 | bytes 128 | tf_op jit(solution)/shard_map/psum | solution.py:116
  278.4 1.5 broadcast_select_fusion
  283.1 27.8 %all-reduce.11.cloned.1.call-done = f32[4,17280]{1,0:T(4,128)} async-done(((f32[4,17280]{1,0:T(4,128)}), f32[4,17280]{1,0:T(4,128)}) %all-reduce.11.cloned.1.call-update) | async-done | bytes 276496 | tf_op jit(solution)/shard_map/psum | solution.py:32
  310.9 2.3 fusion.118
  313.3 11.7 %psum.94 = f32[4,4]{0,1:T(4,128)S(1)} all-reduce(f32[4,4]{0,1:T(4,128)S(1)} %fusion.118), channel_id=1, replica_groups=mesh['member'=2,'vec'=4,'band'=4] {'band'}, use_global_device_ids=true, to_apply=%region_15.18 | all-reduce | flops 16 | bytes 128 | tf_op jit(solution)/shard_map/psum | solution.py:113
  327.7 1.7 fusion.60
  329.4 1.3 fusion.119
  330.7 8.4 %psum.95 = f32[4,4]{0,1:T(4,128)S(1)} all-reduce(f32[4,4]{0,1:T(4,128)S(1)} %fusion.119), channel_id=1, replica_groups=mesh['member'=2,'vec'=4,'band'=4] {'band'}, use_global_device_ids=true, to_apply=%region_16.19 | all-reduce | flops 16 | bytes 128 | tf_op jit(solution)/shard_map/psum | solution.py:116
  339.1 0.8 fusion.7
  339.9 1.1 reshape.65
  (118 shorter events, 24.0 us)
Async XLA Ops:
  7.2 10.8 %copy-start = (f32[4,3,4,1440]{3,2,1,0:T(4,128)S(1)}, f32[4,3,4,1440]{3,2,1,0:T(4,128)}, u32[]{:S(2)}) copy-start(f32[4,3,4,1440]{3,2,1,0:T(4,128)} %param.9) | copy-start | bytes 829444
  7.2 10.9 %copy-start.1 = (f32[4,4,1440]{2,1,0:T(4,128)S(1)}, f32[4,4,1440]{2,1,0:T(4,128)}, u32[]{:S(2)}) copy-start(f32[4,4,1440]{2,1,0:T(4,128)} %param.10) | copy-start | bytes 276484
  7.2 123.4 %all-reduce.5.cloned.1.call-start = ((), (), s32[]{:S(2)}) async-start(), calls=%async_computation | async-start | bytes 552960 | tf_op jit(solution)/shard_map/psum | solution.py:32
  9.1 14.1 %collective-permute-start = (f32[4,3,1,1440]{3,2,1,0:T(1,128)}, f32[4,3,1,1440]{3,2,1,0:T(1,128)S(1)}, u32[]{:S(2)}, u32[]{:S(2)}) collective-permute-start(f32[4,3,1,1440]{3,2,1,0:T(1,128)} %get-tuple-element.171), channel_id=1, source_target_pairs={{1,0},{2,1},{3,2},{5,4},{6,5},{7,6},{9,8},{10,9},{11,10},{13,12},{... | collective-permute-start | bytes 207368 | tf_op jit(solution)/shard_map/ppermute | solution.py:25
  10.4 12.8 %collective-permute-start.1 = (f32[4,3,1,1440]{3,2,1,0:T(1,128)}, f32[4,3,1,1440]{3,2,1,0:T(1,128)S(1)}, u32[]{:S(2)}, u32[]{:S(2)}) collective-permute-start(f32[4,3,1,1440]{3,2,1,0:T(1,128)} %get-tuple-element.172), channel_id=1, source_target_pairs={{0,1},{1,2},{2,3},{4,5},{5,6},{6,7},{8,9},{9,10},{10,11},{12,13},{... | collective-permute-start | bytes 207368 | tf_op jit(solution)/shard_map/ppermute | solution.py:22
  21.2 0.7 copy-start.4
  23.2 0.6 copy-start.2
  23.2 0.6 copy-start.3
  26.0 6.2 %collective-permute-start.2 = (f32[4,3,1,1440]{3,2,1,0:T(1,128)S(1)}, f32[4,3,1,1440]{3,2,1,0:T(1,128)S(1)}, u32[]{:S(2)}, u32[]{:S(2)}) collective-permute-start(f32[4,3,1,1440]{3,2,1,0:T(1,128)S(1)} %get-tuple-element.165), channel_id=1, source_target_pairs={{1,0},{2,1},{3,2},{5,4},{6,5},{7,6},{9,8},{10,9},{11,10},{13,12},{... | collective-permute-start | bytes 207368 | tf_op jit(solution)/shard_map/ppermute | solution.py:25
  27.3 6.5 %collective-permute-start.3 = (f32[4,3,1,1440]{3,2,1,0:T(1,128)S(1)}, f32[4,3,1,1440]{3,2,1,0:T(1,128)S(1)}, u32[]{:S(2)}, u32[]{:S(2)}) collective-permute-start(f32[4,3,1,1440]{3,2,1,0:T(1,128)S(1)} %get-tuple-element.166), channel_id=1, source_target_pairs={{0,1},{1,2},{2,3},{4,5},{5,6},{6,7},{8,9},{9,10},{10,11},{12,13},{... | collective-permute-start | bytes 207368 | tf_op jit(solution)/shard_map/ppermute | solution.py:22
  34.9 6.6 %collective-permute-start.4 = (f32[4,3,1,1440]{3,2,1,0:T(1,128)S(1)}, f32[4,3,1,1440]{3,2,1,0:T(1,128)S(1)}, u32[]{:S(2)}, u32[]{:S(2)}) collective-permute-start(f32[4,3,1,1440]{3,2,1,0:T(1,128)S(1)} %get-tuple-element.159), channel_id=1, source_target_pairs={{1,0},{2,1},{3,2},{5,4},{6,5},{7,6},{9,8},{10,9},{11,10},{13,12},{... | collective-permute-start | bytes 207368 | tf_op jit(solution)/shard_map/ppermute | solution.py:25
  36.2 6.9 %collective-permute-start.5 = (f32[4,3,1,1440]{3,2,1,0:T(1,128)S(1)}, f32[4,3,1,1440]{3,2,1,0:T(1,128)S(1)}, u32[]{:S(2)}, u32[]{:S(2)}) collective-permute-start(f32[4,3,1,1440]{3,2,1,0:T(1,128)S(1)} %get-tuple-element.160), channel_id=1, source_target_pairs={{0,1},{1,2},{2,3},{4,5},{5,6},{6,7},{8,9},{9,10},{10,11},{12,13},{... | collective-permute-start | bytes 207368 | tf_op jit(solution)/shard_map/ppermute | solution.py:22
  44.2 6.6 %collective-permute-start.6 = (f32[4,3,1,1440]{3,2,1,0:T(1,128)S(1)}, f32[4,3,1,1440]{3,2,1,0:T(1,128)S(1)}, u32[]{:S(2)}, u32[]{:S(2)}) collective-permute-start(f32[4,3,1,1440]{3,2,1,0:T(1,128)S(1)} %get-tuple-element.153), channel_id=1, source_target_pairs={{1,0},{2,1},{3,2},{5,4},{6,5},{7,6},{9,8},{10,9},{11,10},{13,12},{... | collective-permute-start | bytes 207368 | tf_op jit(solution)/shard_map/ppermute | solution.py:25
  45.5 6.9 %collective-permute-start.7 = (f32[4,3,1,1440]{3,2,1,0:T(1,128)S(1)}, f32[4,3,1,1440]{3,2,1,0:T(1,128)S(1)}, u32[]{:S(2)}, u32[]{:S(2)}) collective-permute-start(f32[4,3,1,1440]{3,2,1,0:T(1,128)S(1)} %get-tuple-element.154), channel_id=1, source_target_pairs={{0,1},{1,2},{2,3},{4,5},{5,6},{6,7},{8,9},{9,10},{10,11},{12,13},{... | collective-permute-start | bytes 207368 | tf_op jit(solution)/shard_map/ppermute | solution.py:22
  53.6 6.6 %collective-permute-start.8 = (f32[4,3,1,1440]{3,2,1,0:T(1,128)S(1)}, f32[4,3,1,1440]{3,2,1,0:T(1,128)S(1)}, u32[]{:S(2)}, u32[]{:S(2)}) collective-permute-start(f32[4,3,1,1440]{3,2,1,0:T(1,128)S(1)} %get-tuple-element.147), channel_id=1, source_target_pairs={{1,0},{2,1},{3,2},{5,4},{6,5},{7,6},{9,8},{10,9},{11,10},{13,12},{... | collective-permute-start | bytes 207368 | tf_op jit(solution)/shard_map/ppermute | solution.py:25
  54.9 6.9 %collective-permute-start.9 = (f32[4,3,1,1440]{3,2,1,0:T(1,128)S(1)}, f32[4,3,1,1440]{3,2,1,0:T(1,128)S(1)}, u32[]{:S(2)}, u32[]{:S(2)}) collective-permute-start(f32[4,3,1,1440]{3,2,1,0:T(1,128)S(1)} %get-tuple-element.148), channel_id=1, source_target_pairs={{0,1},{1,2},{2,3},{4,5},{5,6},{6,7},{8,9},{9,10},{10,11},{12,13},{... | collective-permute-start | bytes 207368 | tf_op jit(solution)/shard_map/ppermute | solution.py:22
  63.1 6.6 %collective-permute-start.10 = (f32[4,3,1,1440]{3,2,1,0:T(1,128)S(1)}, f32[4,3,1,1440]{3,2,1,0:T(1,128)S(1)}, u32[]{:S(2)}, u32[]{:S(2)}) collective-permute-start(f32[4,3,1,1440]{3,2,1,0:T(1,128)S(1)} %get-tuple-element.141), channel_id=1, source_target_pairs={{1,0},{2,1},{3,2},{5,4},{6,5},{7,6},{9,8},{10,9},{11,10},{13,12},{... | collective-permute-start | bytes 207368 | tf_op jit(solution)/shard_map/ppermute | solution.py:25
  64.4 6.9 %collective-permute-start.11 = (f32[4,3,1,1440]{3,2,1,0:T(1,128)S(1)}, f32[4,3,1,1440]{3,2,1,0:T(1,128)S(1)}, u32[]{:S(2)}, u32[]{:S(2)}) collective-permute-start(f32[4,3,1,1440]{3,2,1,0:T(1,128)S(1)} %get-tuple-element.142), channel_id=1, source_target_pairs={{0,1},{1,2},{2,3},{4,5},{5,6},{6,7},{8,9},{9,10},{10,11},{12,13},{... | collective-permute-start | bytes 207368 | tf_op jit(solution)/shard_map/ppermute | solution.py:22
  72.5 6.6 %collective-permute-start.12 = (f32[4,3,1,1440]{3,2,1,0:T(1,128)S(1)}, f32[4,3,1,1440]{3,2,1,0:T(1,128)S(1)}, u32[]{:S(2)}, u32[]{:S(2)}) collective-permute-start(f32[4,3,1,1440]{3,2,1,0:T(1,128)S(1)} %get-tuple-element.135), channel_id=1, source_target_pairs={{1,0},{2,1},{3,2},{5,4},{6,5},{7,6},{9,8},{10,9},{11,10},{13,12},{... | collective-permute-start | bytes 207368 | tf_op jit(solution)/shard_map/ppermute | solution.py:25
  73.8 6.9 %collective-permute-start.13 = (f32[4,3,1,1440]{3,2,1,0:T(1,128)S(1)}, f32[4,3,1,1440]{3,2,1,0:T(1,128)S(1)}, u32[]{:S(2)}, u32[]{:S(2)}) collective-permute-start(f32[4,3,1,1440]{3,2,1,0:T(1,128)S(1)} %get-tuple-element.136), channel_id=1, source_target_pairs={{0,1},{1,2},{2,3},{4,5},{5,6},{6,7},{8,9},{9,10},{10,11},{12,13},{... | collective-permute-start | bytes 207368 | tf_op jit(solution)/shard_map/ppermute | solution.py:22
  82.0 6.6 %collective-permute-start.14 = (f32[4,3,1,1440]{3,2,1,0:T(1,128)S(1)}, f32[4,3,1,1440]{3,2,1,0:T(1,128)S(1)}, u32[]{:S(2)}, u32[]{:S(2)}) collective-permute-start(f32[4,3,1,1440]{3,2,1,0:T(1,128)S(1)} %get-tuple-element.129), channel_id=1, source_target_pairs={{1,0},{2,1},{3,2},{5,4},{6,5},{7,6},{9,8},{10,9},{11,10},{13,12},{... | collective-permute-start | bytes 207368 | tf_op jit(solution)/shard_map/ppermute | solution.py:25
  83.3 6.9 %collective-permute-start.15 = (f32[4,3,1,1440]{3,2,1,0:T(1,128)S(1)}, f32[4,3,1,1440]{3,2,1,0:T(1,128)S(1)}, u32[]{:S(2)}, u32[]{:S(2)}) collective-permute-start(f32[4,3,1,1440]{3,2,1,0:T(1,128)S(1)} %get-tuple-element.130), channel_id=1, source_target_pairs={{0,1},{1,2},{2,3},{4,5},{5,6},{6,7},{8,9},{9,10},{10,11},{12,13},{... | collective-permute-start | bytes 207368 | tf_op jit(solution)/shard_map/ppermute | solution.py:22
  90.8 0.7 copy-start.5
  95.2 95.4 %all-reduce.7.cloned.1.call-start = ((), (), s32[]{:S(2)}) async-start(), calls=%async_computation.1 | async-start | bytes 552960 | tf_op jit(solution)/shard_map/psum | solution.py:32
  159.6 91.2 %all-reduce.9.cloned.1.call-start = ((), (), s32[]{:S(2)}) async-start(), calls=%async_computation.2 | async-start | bytes 552960 | tf_op jit(solution)/shard_map/psum | solution.py:32
  219.9 91.0 %all-reduce.11.cloned.1.call-start = ((), (), s32[]{:S(2)}) async-start(), calls=%async_computation.3 | async-start | bytes 552960 | tf_op jit(solution)/shard_map/psum | solution.py:32
Sparse Core Ops, SparseCore 0:
  95.4 35.1 all-reduce.4
  159.7 30.8 all-reduce.6
  220.0 30.8 all-reduce.8
  280.1 30.8 all-reduce.10
where the time goes:
time: 349 us; the launch traced here: 348 us
  waiting for transfers between devices  132 us (38%)
  blocking collectives  80.3 us (23%)
  starting transfers between devices  50.2 us (14%)
  matrix products  29.2 us (8%)
  between operations  21.9 us (6%)
  other arithmetic  21.5 us (6%)
  local copies, waits for them, and re-layouts  13.3 us (4%)
    psum x4, waiting for transfers between devices, broadcast(): return lax.psum(kept, axis)  119 us
    psum x4, blocking collectives, on_device(): lax.psum(jnp.dot(panel, panel.T, precision=lax.Precision.HIGHEST), 'band')  46.9 us
    ppermute x8, starting transfers between devices, extended(): lax.ppermute(lax.slice_in_dim(block, block.shape[dim] - width, None, axis...  39.7 us
    psum x4, blocking collectives, on_device(): lax.psum(jnp.dot(flat, ortho.T, precision=lax.Precision.HIGHEST), 'band')  33.4 us
    ppermute x8, waiting for transfers between devices, extended(): lax.ppermute(lax.slice_in_dim(block, block.shape[dim] - width, None, axis...  11 us
    ppermute x8, starting transfers between devices, extended(): lax.ppermute(lax.slice_in_dim(block, 0, width, axis=dim), axis, backward)  10.3 us
    dot_general x4, matrix products, on_device(): jnp.dot(panel, panel.T, precision=lax.Precision.HIGHEST)  9.4 us
  transfers between devices with their start and end apart: 20, of which 18 were waited for; matrix products, arithmetic and copies ran while one was open for 3% of the time, Pallas kernels for 0%

commit v1 on v0

--- a/solution.py
+++ b/solution.py
@@ -1,8 +1,14 @@
 import math
+
+import functools
 
 import jax
 import jax.numpy as jnp
+import ml_dtypes
+import numpy as np
 from jax import lax
+from jax.experimental import pallas as pl
+from jax.experimental.pallas import tpu as pltpu
 from jax.sharding import PartitionSpec as P
 
 KMAX = 128
@@ -120,9 +126,310 @@
     return (flat.reshape(state.shape), growth)
 
 
+MESH = pl.DeviceIdType.MESH
+HIGHEST = lax.Precision.HIGHEST
+GROUP = 4
+NUM = GROUP * GROUP
+
+
+def split_table(nlon, kmax, width):
+    waves = np.arange(kmax)[:, None]
+    phase = (waves * np.arange(nlon)[None, :] % nlon) * (2.0 * np.pi / nlon)
+    scale = np.where(waves == 0, np.sqrt(1.0 / nlon), np.sqrt(2.0 / nlon))
+    table = np.concatenate([np.cos(phase) * scale, np.sin(phase) * np.sqrt(2.0 / nlon)], 0)
+    table = table.astype(np.float32)
+    high = table.astype(ml_dtypes.bfloat16)
+    low = (table - high.astype(np.float32)).astype(ml_dtypes.bfloat16)
+    rows = ((0, width - nlon), (0, 0))
+    return np.stack([high, low]), np.stack([np.pad(high.T, rows), np.pad(low.T, rows)])
+
+
+def halves(value):
+    high = value.astype(jnp.bfloat16)
+    return high, (value - high.astype(jnp.float32)).astype(jnp.bfloat16)
+
+
+def dot_split(value, table_ref):
+    high, low = halves(value)
+    dot = functools.partial(jnp.dot, preferred_element_type=jnp.float32)
+    return dot(high, table_ref[0]) + (dot(low, table_ref[0]) + dot(high, table_ref[1]))
+
+
+def dot_full(left, right):
+    return jnp.dot(left, right, precision=HIGHEST, preferred_element_type=jnp.float32)
+
+
+def iota(shape, dim):
+    return lax.broadcasted_iota(jnp.int32, shape, dim)
+
+
+def tend_rows(h, u, v, coef):
+    neg_u, neg_v, neg_h, rot = coef
+    rows, width = h.shape
+    row = iota((rows, width), 0)
+
+    def along_x(z):
+        return pltpu.roll(z, width - 1, 1) - pltpu.roll(z, 1, 1)
+
+    def along_y(z):
+        above = jnp.where(row == rows - 1, 0.0, pltpu.roll(z, rows - 1, 0))
+        below = jnp.where(row == 0, 0.0, pltpu.roll(z, 1, 0))
+        return above - below
+
+    xh, xu, xv = along_x(h), along_x(u), along_x(v)
+    yh, yu, yv = along_y(h), along_y(u), along_y(v)
+    th = neg_u * xh + neg_v * yh + neg_h * (xu + yv)
+    tu = neg_u * xu + neg_v * yu - 0.5 * xh + rot * v
+    tv = neg_u * xv + neg_v * yv - 0.5 * yh - rot * u
+    return th, tu, tv
+
+
+def step_rows(x, coef):
+    k = tend_rows(*x, coef)
+    total = k
+    for scale, weight in ((half_dt, 2.0), (half_dt, 2.0), (step_dt, 1.0)):
+        k = tend_rows(*[a + scale * b for a, b in zip(x, k)], coef)
+        total = [a + weight * b for a, b in zip(total, k)]
+    return [a + sixth_dt * b for a, b in zip(x, total)]
+
+
+def whole_kernel(
+    nlon, width, size,
+    order_ref, cut_ref, vec_hbm, flow_hbm, fwd_hbm, inv_hbm,
+    out_ref, growth_ref,
+    vbuf, fbuf, fwd, inv, xs, fs, sbuf, cs, gsend, gbuf, nb,
+    local_sem, vsend, vrecv, fsend, frecv, gosend, gorecv, csend, crecv, asend, arecv, msend, mrecv,
+):
+    b = lax.axis_index("band")
+    v = lax.axis_index("vec")
+
+    def peer(k):
+        return lax.rem(b + k // GROUP, GROUP), lax.rem(v + k % GROUP, GROUP)
+
+    def remote(src, dst, send, recv, b2, v2):
+        return pltpu.make_async_remote_copy(
+            src_ref=src, dst_ref=dst, send_sem=send, recv_sem=recv,
+            device_id={"band": b2, "vec": v2}, device_id_type=MESH,
+        )
+
+    own = [
+        pltpu.make_async_copy(flow_hbm.at[v], fbuf.at[v, b], local_sem.at[0]),
+        pltpu.make_async_copy(vec_hbm.at[b], vbuf.at[b], local_sem.at[1]),
+        pltpu.make_async_copy(fwd_hbm, fwd, local_sem.at[2]),
+        pltpu.make_async_copy(inv_hbm, inv, local_sem.at[3]),
+    ]
+    for copy in own:
+        copy.start()
+
+    barrier = pltpu.get_barrier_semaphore()
+    for k in range(1, NUM):
+        b2, v2 = peer(k)
+        pl.semaphore_signal(barrier, inc=1, device_id={"band": b2, "vec": v2}, device_id_type=MESH)
+    pl.semaphore_wait(barrier, NUM - 1)
+
+    flow_copies, vec_copies = [], []
+    for k in range(1, GROUP):
+        b2 = lax.rem(b + k, GROUP)
+        flow_copies.append(
+            remote(flow_hbm.at[v], fbuf.at[v, b], fsend.at[k], frecv.at[k], b2, v)
+        )
+        flow_copies[-1].start()
+    for k in range(1, GROUP):
+        b2 = lax.rem(b + k, GROUP)
+        vec_copies.append(remote(vec_hbm.at[b2], vbuf.at[b], vsend.at[k], vrecv.at[k], b2, v))
+        vec_copies[-1].start()
+
+    lane = iota((NUM, 128), 1)
+    row = iota((NUM, 128), 0)
+
+    def placed(at):
+        turn = at // GROUP
+        block = jnp.where(
+            turn == 0, order_ref[0],
+            jnp.where(turn == 1, order_ref[1], jnp.where(turn == 2, order_ref[2], order_ref[3])),
+        )
+        return GROUP * block + at % GROUP
+
+    permute = (lane == placed(row)).astype(jnp.float32)
+    lane_big = iota((128, 128), 1)
+    row_big = iota((128, 128), 0)
+    unpack = (
+        (row_big % NUM == placed(lane_big - NUM)) & (lane_big >= NUM) & (lane_big < 2 * NUM)
+    ).astype(jnp.float32)
+    diagonal = lane // NUM == row % 8
+    own_rows = (placed(lane[:8]) == GROUP * v + row[:8]) & (lane[:8] < NUM) & (row[:8] < GROUP)
+    own_rows = own_rows.astype(jnp.float32)
+    wave = iota((NUM, 2 * KMAX), 1) % KMAX
+    wave_row = iota((NUM, 2 * KMAX), 0)
+    cut = jnp.zeros((NUM, 2 * KMAX), jnp.int32)
+    for r in range(NUM):
+        cut = jnp.where(wave_row == r, cut_ref[r], cut)
+    keep = wave <= cut
+
+    own[0].wait()
+    for copy in flow_copies:
+        copy.wait_recv()
+    forwards = []
+    for k in range(1, GROUP):
+        v2 = lax.rem(v + k, GROUP)
+        forwards.append(remote(fbuf.at[v], fbuf.at[v], gosend.at[k], gorecv.at[k], b, v2))
+        forwards[-1].start()
+
+    own[1].wait()
+    for copy in vec_copies:
+        copy.wait_recv()
+    for copy in forwards:
+        copy.wait_recv()
+
+    extra = width - nlon
+    for f in range(3):
+        for band in range(GROUP):
+            xs[f, GROUP * band : GROUP * (band + 1), :nlon] = vbuf[band, f]
+    for f in range(GROUP):
+        for band in range(GROUP):
+            fs[f, GROUP * band : GROUP * (band + 1), :nlon] = fbuf[f, band]
+
+    def wrapped(z):
+        return jnp.concatenate([z, z[:, : extra // 2], z[:, nlon - extra // 2 :]], axis=1)
+
+    x = [wrapped(xs[f, :, :nlon]) for f in range(3)]
+    speed_x, speed_y, deep, turning = [wrapped(fs[f, :, :nlon]) for f in range(GROUP)]
+    coef = (-0.5 * speed_x, -0.5 * speed_y, -0.5 - 0.25 * deep, 0.5 * turning)
+    for _ in range(2):
+        x = step_rows(x, coef)
+
+    own[2].wait()
+    modes = dot_split(jnp.concatenate(x, axis=0), fwd)
+    for f in range(3):
+        kept = jnp.where(keep, modes[NUM * f : NUM * (f + 1)], 0.0)
+        sbuf[:, 0, 2 * KMAX * f : 2 * KMAX * (f + 1)] = kept
+
+    me = GROUP * v + b
+    mode_copies = []
+    for k in range(1, NUM):
+        b2, v2 = peer(k)
+        mode_copies.append(
+            remote(sbuf.at[GROUP * b2 + v2], cs.at[v2, me], csend.at[k], crecv.at[k], b2, v2)
+        )
+        mode_copies[-1].start()
+    cs[v, me] = sbuf[GROUP * b + v]
+    for copy in mode_copies:
+        copy.wait_recv()
+
+    gathers = []
+    for k in range(1, GROUP):
+        v2 = lax.rem(v + k, GROUP)
+        gathers.append(remote(cs.at[v], cs.at[v], asend.at[k], arecv.at[k], b, v2))
+
+    part = cs[v].reshape(NUM, 6 * KMAX)
+    tiled = jnp.concatenate([part] * 8, axis=0)
+    product = lax.dot_general(
+        part, tiled, (((1,), (1,)), ((), ())), precision=HIGHEST,
+        preferred_element_type=jnp.float32,
+    )
+    product = jnp.where(diagonal, product, 0.0)
+    gsend[0:1, :] = jnp.sum(product[:8], axis=0, keepdims=True)
+    gsend[1:2, :] = jnp.sum(product[8:], axis=0, keepdims=True)
+    gram_copies = []
+    for k in range(1, NUM):
+        b2, v2 = peer(k)
+        gram_copies.append(remote(gsend, gbuf.at[me], msend.at[k], mrecv.at[k], b2, v2))
+        gram_copies[-1].start()
+    for copy in gathers:
+        copy.start()
+    gbuf[me] = gsend[...]
+    for copy in gram_copies:
+        copy.wait_recv()
+    gram = gbuf[0]
+    for k in range(1, NUM):
+        gram = gram + gbuf[k]
+    gram = gram * (1.0 / size)
+    spread = jnp.concatenate(
+        [jnp.broadcast_to(gram[i : i + 1], (8, 128)) for i in range(2)], axis=0
+    )
+    spread = jnp.where(diagonal, spread, 0.0)
+    grid = dot_full(permute[:, :NUM], dot_full(spread, unpack))
+    grid = jnp.where(lane < NUM, permute, grid)
+    for s in range(NUM - 1):
+        col = grid[:, NUM + s : NUM + s + 1]
+        factor = col / grid[s : s + 1, NUM + s : NUM + s + 1]
+        grid = grid - jnp.where(row > s, factor * grid[s : s + 1, :], 0.0)
+    pivot = jnp.sum(jnp.where(lane == row + NUM, grid, 0.0), axis=1, keepdims=True)
+    root = jnp.sqrt(pivot)
+    logs = jnp.broadcast_to(jnp.log(root), (NUM, 128))
+    mix = jnp.where(lane < NUM, grid / root, logs)
+    mix = dot_full(own_rows[:, :NUM], mix)
+    for i in range(GROUP):
+        growth_ref[i] = mix[i, NUM]
+
+    for copy in gathers:
+        copy.wait_recv()
+    for r in range(GROUP):
+        fresh = dot_full(mix[:, :NUM], cs[r].reshape(NUM, 6 * KMAX))
+        for i in range(GROUP):
+            for f in range(3):
+                at = 12 * i + GROUP * f + r
+                nb[at : at + 1, :] = fresh[i : i + 1, 2 * KMAX * f : 2 * KMAX * (f + 1)]
+    own[3].wait()
+    result = dot_split(nb[...], inv)
+    for i in range(GROUP):
+        for f in range(3):
+            at = 12 * i + GROUP * f
+            out_ref[i, f] = result[at : at + GROUP]
+
+    for copy in flow_copies + vec_copies + forwards + mode_copies + gathers + gram_copies:
+        copy.wait_send()
+
+
+def on_group(vectors, flow, band_cut, order):
+    nlon = vectors.shape[3]
+    width = -(-nlon // 128) * 128
+    inv, fwd = split_table(nlon, KMAX, width)
+    any_spec = pl.BlockSpec(memory_space=pl.ANY)
+    smem = pl.BlockSpec(memory_space=pltpu.SMEM)
+    dma = pltpu.SemaphoreType.DMA
+    size = float(3 * NUM * nlon)
+    return tuple(pl.pallas_call(
+        functools.partial(whole_kernel, nlon, width, size),
+        out_shape=[
+            jax.ShapeDtypeStruct(vectors.shape, jnp.float32),
+            jax.ShapeDtypeStruct((GROUP,), jnp.float32),
+        ],
+        in_specs=[smem, smem, any_spec, any_spec, any_spec, any_spec],
+        out_specs=[pl.BlockSpec(memory_space=pltpu.VMEM), smem],
+        scratch_shapes=[
+            pltpu.VMEM((GROUP, 3, GROUP, nlon), jnp.float32),
+            pltpu.VMEM((GROUP, GROUP, GROUP, nlon), jnp.float32),
+            pltpu.VMEM(fwd.shape, jnp.bfloat16),
+            pltpu.VMEM(inv.shape, jnp.bfloat16),
+            pltpu.VMEM((3, NUM, width), jnp.float32),
+            pltpu.VMEM((GROUP, NUM, width), jnp.float32),
+            pltpu.VMEM((NUM, 1, 6 * KMAX), jnp.float32),
+            pltpu.VMEM((GROUP, NUM, 1, 6 * KMAX), jnp.float32),
+            pltpu.VMEM((2, 128), jnp.float32),
+            pltpu.VMEM((NUM, 2, 128), jnp.float32),
+            pltpu.VMEM((3 * NUM, 2 * KMAX), jnp.float32),
+            dma((4,)),
+            dma((GROUP,)), dma((GROUP,)), dma((GROUP,)), dma((GROUP,)), dma((GROUP,)), dma((GROUP,)),
+            dma((NUM,)), dma((NUM,)), dma((GROUP,)), dma((GROUP,)), dma((NUM,)), dma((NUM,)),
+        ],
+        compiler_params=pltpu.CompilerParams(
+            collective_id=0, has_side_effects=True, vmem_limit_bytes=40 << 20
+        ),
+    )(order, band_cut, vectors, flow, jnp.asarray(fwd), jnp.asarray(inv)))
+
+
 def solution(mesh):
     in_specs = (P(("member", "vec"), None, "band", None), P(None, "band", None), P(), P())
     out_specs = (P(("member", "vec"), None, "band", None), P(("member", "vec")))
+
+    def body(vectors, flow, band_cut, order):
+        rows = mesh.shape["band"] * vectors.shape[2]
+        square = (mesh.shape["band"], mesh.shape["vec"], vectors.shape[0], vectors.shape[2])
+        if rows == band_cut.shape[0] and square == (GROUP,) * 4:
+            return on_group(vectors, flow, band_cut, order)
+        return on_device(vectors, flow, band_cut, order)
+
     return jax.shard_map(
-        on_device, mesh=mesh, in_specs=in_specs, out_specs=out_specs, check_vma=False
+        body, mesh=mesh, in_specs=in_specs, out_specs=out_specs, check_vma=False
     )

time: 349 us -> 41.6 us (0.12)
  waiting for transfers between devices: 132 us -> 0 us
  blocking collectives: 80.3 us -> 0 us
  starting transfers between devices: 50.2 us -> 0 us
  Pallas kernels: 0 us -> 33.5 us
  matrix products: 29.2 us -> 0 us
  other arithmetic: 21.5 us -> 0 us
  between operations: 21.9 us -> 0.65 us
  local copies, waits for them, and re-layouts: 13.3 us -> 7.2 us
    psum x4 -> x0, waiting for transfers between devices: 119 us -> none  [broadcast(): return lax.psum(kept, axis)]
    psum x8 -> x0, blocking collectives: 80.3 us -> none  [the longest x4 46.9 us: on_device(): lax.psum(jnp.dot(panel, panel.T, precision=lax.Precision.HIGHEST), 'band')]
    ppermute x16 -> x0, starting transfers between devices: 50.1 us -> none  [the longest x8 39.7 us: extended(): lax.ppermute(lax.slice_in_dim(block, block.shape[dim] - width, None, axis...]
    pallas_call x0 -> x1, Pallas kernels: none -> 33.5 us  [on_group(): pl.pallas_call(functools.partial(whole_kernel, nlon, width, size), out_sh...]
    dot_general x14 -> x0, matrix products: 22.5 us -> none  [the longest x4 9.4 us: on_device(): jnp.dot(panel, panel.T, precision=lax.Precision.HIGHEST)]
    ppermute x16 -> x0, waiting for transfers between devices: 13 us -> none  [the longest x8 11 us: extended(): lax.ppermute(lax.slice_in_dim(block, block.shape[dim] - width, None, axis...]
    another operation x20 -> x0, other arithmetic: 8.09 us -> none  [the longest x12 4.14 us: on_device(): lower = jnp.linalg.cholesky(gram)]
    mul x10 -> x0, other arithmetic: 8.06 us -> none  [the longest x8 4.93 us: tendency(): dx = 0.5 * (jnp.roll(inner, -1, 3) - jnp.roll(inner, 1, 3))]
  transfers between devices with their start and end apart: 20 -> 0, of which waited for: 18 -> 0; matrix products, arithmetic and copies ran while one was open for 3% -> 0% of each run, Pallas kernels for 0% -> 0%
where the time goes in v1:
time: 41.6 us; the launch traced here: 41.4 us
  Pallas kernels  33.5 us (81%)
  local copies, waits for them, and re-layouts  7.2 us (17%)
  between operations  0.65 us (2%)
    pallas_call x1, Pallas kernels, on_group(): pl.pallas_call(functools.partial(whole_kernel, nlon, width, size), out_sh...  33.5 us
    unnamed x14, local copies, waits for them, and re-layouts  7.2 us

profile of v1, /device:TPU:0, one launch (start us, length us, event | category | flops | bytes accessed | tf_op | source)
XLA Modules:
  0.0 41.4 jit_solution(14571608037305128937)
XLA Ops:
  0.6 0.0 copy-start
  0.6 1.4 %copy-done = bf16[2,256,1440]{2,1,0:T(8,128)(2,1)S(1)} copy-done((bf16[2,256,1440]{2,1,0:T(8,128)(2,1)S(1)}, bf16[2,256,1440]{2,1,0:T(8,128)(2,1)}, u32[]{:S(2)}) %copy-start) | copy-done | bytes 1474584
  2.0 0.0 copy-start.1
  2.0 1.4 %copy-done.1 = bf16[2,1536,256]{2,1,0:T(8,128)(2,1)S(1)} copy-done((bf16[2,1536,256]{2,1,0:T(8,128)(2,1)S(1)}, bf16[2,1536,256]{2,1,0:T(8,128)(2,1)}, u32[]{:S(2)}) %copy-start.1) | copy-done | bytes 1572888
  3.5 0.0 copy-start.2
  3.5 1.0 %copy-done.2 = f32[4,3,4,1440]{3,2,1,0:T(4,128)S(1)} copy-done((f32[4,3,4,1440]{3,2,1,0:T(4,128)S(1)}, f32[4,3,4,1440]{3,2,1,0:T(4,128)}, u32[]{:S(2)}) %copy-start.2) | copy-done | bytes 276504
  4.4 0.0 copy-start.3
  4.4 0.9 %copy-done.3 = f32[4,4,1440]{2,1,0:T(4,128)S(1)} copy-done((f32[4,4,1440]{2,1,0:T(4,128)S(1)}, f32[4,4,1440]{2,1,0:T(4,128)}, u32[]{:S(2)}) %copy-start.3) | copy-done | bytes 92184
  5.3 0.0 copy-start.4
  5.3 0.7 %copy-done.4 = s32[4]{0:T(128)S(1)} copy-done((s32[4]{0:T(128)S(1)}, s32[4]{0:T(128)}, u32[]{:S(2)}) %copy-start.4) | copy-done | bytes 40
  6.0 0.0 copy-start.5
  6.0 0.7 %copy-done.5 = s32[16]{0:T(128)S(1)} copy-done((s32[16]{0:T(128)S(1)}, s32[16]{0:T(128)}, u32[]{:S(2)}) %copy-start.5) | copy-done | bytes 88
  6.6 33.5 %shard_map.77 = (f32[4,3,4,1440]{3,2,1,0:T(4,128)S(1)}, f32[4]{0:T(128)S(1)}) custom-call(s32[4]{0:T(128)S(1)} %copy-done.4, s32[16]{0:T(128)S(1)} %copy-done.5, f32[4,3,4,1440]{3,2,1,0:T(4,128)S(1)} %copy-done.2, f32[4,4,1440]{2,1,0:T(4,128)S(1)} %copy-done.3, bf16[2,1536,256]{2,1,0:T(8,128)(2,1)S(1)} %copy-done.1, bf16[2,256,1440]{2,1,0:T(8,128)(2,1)S(1)} %copy-done), custom_call_target="tpu_custom_call" | custom-call | tf_op jit(solution)/shard_map/pallas_call | solution.py:392
  40.2 0.7 %copy.10 = f32[4,3,4,1440]{3,2,1,0:T(4,128)} copy(f32[4,3,4,1440]{3,2,1,0:T(4,128)S(1)} %get-tuple-element.4) | data formatting | bytes 552960
  40.9 0.5 %copy.11 = f32[4]{0:T(128)} copy(f32[4]{0:T(128)S(1)} %get-tuple-element.5) | data formatting | bytes 32
Async XLA Ops:
  0.6 1.4 %copy-start = (bf16[2,256,1440]{2,1,0:T(8,128)(2,1)S(1)}, bf16[2,256,1440]{2,1,0:T(8,128)(2,1)}, u32[]{:S(2)}) copy-start(bf16[2,256,1440]{2,1,0:T(8,128)(2,1)} %constant.5.clone.inv_hbm) | copy-start | bytes 4423684
  2.0 1.4 %copy-start.1 = (bf16[2,1536,256]{2,1,0:T(8,128)(2,1)S(1)}, bf16[2,1536,256]{2,1,0:T(8,128)(2,1)}, u32[]{:S(2)}) copy-start(bf16[2,1536,256]{2,1,0:T(8,128)(2,1)} %constant.4.clone.fwd_hbm) | copy-start | bytes 4718596
  3.5 1.0 %copy-start.2 = (f32[4,3,4,1440]{3,2,1,0:T(4,128)S(1)}, f32[4,3,4,1440]{3,2,1,0:T(4,128)}, u32[]{:S(2)}) copy-start(f32[4,3,4,1440]{3,2,1,0:T(4,128)} %vec_hbm.1) | copy-start | bytes 829444
  4.4 0.9 %copy-start.3 = (f32[4,4,1440]{2,1,0:T(4,128)S(1)}, f32[4,4,1440]{2,1,0:T(4,128)}, u32[]{:S(2)}) copy-start(f32[4,4,1440]{2,1,0:T(4,128)} %flow_hbm.1) | copy-start | bytes 276484
  5.3 0.7 %copy-start.4 = (s32[4]{0:T(128)S(1)}, s32[4]{0:T(128)}, u32[]{:S(2)}) copy-start(s32[4]{0:T(128)} %order_ref.1) | copy-start | bytes 52
  6.0 0.7 %copy-start.5 = (s32[16]{0:T(128)S(1)}, s32[16]{0:T(128)}, u32[]{:S(2)}) copy-start(s32[16]{0:T(128)} %cut_ref.1) | copy-start | bytes 196

commit v2 on v1

--- a/solution.py
+++ b/solution.py
@@ -195,16 +195,13 @@
 
 def whole_kernel(
     nlon, width, size,
-    order_ref, cut_ref, vec_hbm, flow_hbm, fwd_hbm, inv_hbm,
-    out_ref, growth_ref,
-    vbuf, fbuf, fwd, inv, xs, fs, sbuf, cs, gsend, gbuf, nb,
+    order_hbm, cut_hbm, vec_hbm, flow_hbm, fwd_hbm,
+    nb, mix_ref,
+    order_ref, cut_ref, vbuf, fbuf, fwd, xs, fs, sbuf, cs, gsend, gbuf,
     local_sem, vsend, vrecv, fsend, frecv, gosend, gorecv, csend, crecv, asend, arecv, msend, mrecv,
 ):
     b = lax.axis_index("band")
     v = lax.axis_index("vec")
-
-    def peer(k):
-        return lax.rem(b + k // GROUP, GROUP), lax.rem(v + k % GROUP, GROUP)
 
     def remote(src, dst, send, recv, b2, v2):
         return pltpu.make_async_remote_copy(
@@ -216,29 +213,33 @@
         pltpu.make_async_copy(flow_hbm.at[v], fbuf.at[v, b], local_sem.at[0]),
         pltpu.make_async_copy(vec_hbm.at[b], vbuf.at[b], local_sem.at[1]),
         pltpu.make_async_copy(fwd_hbm, fwd, local_sem.at[2]),
-        pltpu.make_async_copy(inv_hbm, inv, local_sem.at[3]),
+        pltpu.make_async_copy(order_hbm, order_ref, local_sem.at[3]),
+        pltpu.make_async_copy(cut_hbm, cut_ref, local_sem.at[4]),
     ]
     for copy in own:
         copy.start()
 
     barrier = pltpu.get_barrier_semaphore()
-    for k in range(1, NUM):
-        b2, v2 = peer(k)
+    bands = [lax.rem(b + k, GROUP) for k in range(GROUP)]
+    vecs = [lax.rem(v + k, GROUP) for k in range(GROUP)]
+    for b2, v2 in [(b2, v) for b2 in bands[1:]] + [(b, v2) for v2 in vecs[1:]]:
         pl.semaphore_signal(barrier, inc=1, device_id={"band": b2, "vec": v2}, device_id_type=MESH)
-    pl.semaphore_wait(barrier, NUM - 1)
+    pl.semaphore_wait(barrier, 2 * GROUP - 2)
 
     flow_copies, vec_copies = [], []
     for k in range(1, GROUP):
-        b2 = lax.rem(b + k, GROUP)
+        b2 = bands[k]
         flow_copies.append(
             remote(flow_hbm.at[v], fbuf.at[v, b], fsend.at[k], frecv.at[k], b2, v)
         )
         flow_copies[-1].start()
     for k in range(1, GROUP):
-        b2 = lax.rem(b + k, GROUP)
+        b2 = bands[k]
         vec_copies.append(remote(vec_hbm.at[b2], vbuf.at[b], vsend.at[k], vrecv.at[k], b2, v))
         vec_copies[-1].start()
 
+    own[3].wait()
+    own[4].wait()
     lane = iota((NUM, 128), 1)
     row = iota((NUM, 128), 0)
 
@@ -271,7 +272,7 @@
         copy.wait_recv()
     forwards = []
     for k in range(1, GROUP):
-        v2 = lax.rem(v + k, GROUP)
+        v2 = vecs[k]
         forwards.append(remote(fbuf.at[v], fbuf.at[v], gosend.at[k], gorecv.at[k], b, v2))
         forwards[-1].start()
 
@@ -304,45 +305,45 @@
         kept = jnp.where(keep, modes[NUM * f : NUM * (f + 1)], 0.0)
         sbuf[:, 0, 2 * KMAX * f : 2 * KMAX * (f + 1)] = kept
 
-    me = GROUP * v + b
     mode_copies = []
-    for k in range(1, NUM):
-        b2, v2 = peer(k)
-        mode_copies.append(
-            remote(sbuf.at[GROUP * b2 + v2], cs.at[v2, me], csend.at[k], crecv.at[k], b2, v2)
+    for k in range(1, GROUP):
+        b2 = bands[k]
+        rows = pl.ds(pl.multiple_of(GROUP * b2, GROUP), GROUP)
+        mode_copies.append(remote(sbuf.at[rows], cs.at[v, b], csend.at[k], crecv.at[k], b2, v))
+        mode_copies[-1].start()
+    cs[v, b] = sbuf[pl.ds(pl.multiple_of(GROUP * b, GROUP), GROUP)]
+    for copy in mode_copies:
+        copy.wait_recv()
+    gathers = []
+    for k in range(1, GROUP):
+        v2 = vecs[k]
+        gathers.append(remote(cs.at[v], cs.at[v], asend.at[k], arecv.at[k], b, v2))
+        gathers[-1].start()
+    for copy in gathers:
+        copy.wait_recv()
+
+    product = 0.0
+    parts = []
+    for r in range(GROUP):
+        part = cs[:, :, r].reshape(NUM, 6 * KMAX)
+        parts.append(part)
+        tiled = jnp.concatenate([part] * 8, axis=0)
+        product = product + lax.dot_general(
+            part, tiled, (((1,), (1,)), ((), ())), precision=HIGHEST,
+            preferred_element_type=jnp.float32,
         )
-        mode_copies[-1].start()
-    cs[v, me] = sbuf[GROUP * b + v]
-    for copy in mode_copies:
-        copy.wait_recv()
-
-    gathers = []
-    for k in range(1, GROUP):
-        v2 = lax.rem(v + k, GROUP)
-        gathers.append(remote(cs.at[v], cs.at[v], asend.at[k], arecv.at[k], b, v2))
-
-    part = cs[v].reshape(NUM, 6 * KMAX)
-    tiled = jnp.concatenate([part] * 8, axis=0)
-    product = lax.dot_general(
-        part, tiled, (((1,), (1,)), ((), ())), precision=HIGHEST,
-        preferred_element_type=jnp.float32,
-    )
     product = jnp.where(diagonal, product, 0.0)
     gsend[0:1, :] = jnp.sum(product[:8], axis=0, keepdims=True)
     gsend[1:2, :] = jnp.sum(product[8:], axis=0, keepdims=True)
     gram_copies = []
-    for k in range(1, NUM):
-        b2, v2 = peer(k)
-        gram_copies.append(remote(gsend, gbuf.at[me], msend.at[k], mrecv.at[k], b2, v2))
+    for k in range(1, GROUP):
+        b2 = bands[k]
+        gram_copies.append(remote(gsend, gbuf.at[b], msend.at[k], mrecv.at[k], b2, v))
         gram_copies[-1].start()
-    for copy in gathers:
-        copy.start()
-    gbuf[me] = gsend[...]
+    gbuf[b] = gsend[...]
     for copy in gram_copies:
         copy.wait_recv()
-    gram = gbuf[0]
-    for k in range(1, NUM):
-        gram = gram + gbuf[k]
+    gram = (gbuf[0] + gbuf[1]) + (gbuf[2] + gbuf[3])
     gram = gram * (1.0 / size)
     spread = jnp.concatenate(
         [jnp.broadcast_to(gram[i : i + 1], (8, 128)) for i in range(2)], axis=0
@@ -359,64 +360,73 @@
     logs = jnp.broadcast_to(jnp.log(root), (NUM, 128))
     mix = jnp.where(lane < NUM, grid / root, logs)
     mix = dot_full(own_rows[:, :NUM], mix)
-    for i in range(GROUP):
-        growth_ref[i] = mix[i, NUM]
-
-    for copy in gathers:
-        copy.wait_recv()
+    mix_ref[...] = mix
+
     for r in range(GROUP):
-        fresh = dot_full(mix[:, :NUM], cs[r].reshape(NUM, 6 * KMAX))
+        fresh = dot_full(mix[:, :NUM], parts[r])
         for i in range(GROUP):
             for f in range(3):
                 at = 12 * i + GROUP * f + r
                 nb[at : at + 1, :] = fresh[i : i + 1, 2 * KMAX * f : 2 * KMAX * (f + 1)]
-    own[3].wait()
-    result = dot_split(nb[...], inv)
+    for copy in flow_copies + vec_copies + forwards + mode_copies + gathers + gram_copies:
+        copy.wait_send()
+
+
+def final_kernel(nb, mix_ref, inv_ref, out_ref, growth_ref):
+    result = dot_split(nb[...], inv_ref)
     for i in range(GROUP):
+        growth_ref[i] = mix_ref[i, NUM]
         for f in range(3):
             at = 12 * i + GROUP * f
             out_ref[i, f] = result[at : at + GROUP]
-
-    for copy in flow_copies + vec_copies + forwards + mode_copies + gathers + gram_copies:
-        copy.wait_send()
 
 
 def on_group(vectors, flow, band_cut, order):
     nlon = vectors.shape[3]
     width = -(-nlon // 128) * 128
     inv, fwd = split_table(nlon, KMAX, width)
-    any_spec = pl.BlockSpec(memory_space=pl.ANY)
+    any_spec = pl.BlockSpec(memory_space=pltpu.HBM)
     smem = pl.BlockSpec(memory_space=pltpu.SMEM)
+    vmem = pl.BlockSpec(memory_space=pltpu.VMEM)
     dma = pltpu.SemaphoreType.DMA
     size = float(3 * NUM * nlon)
+    fresh, mix = pl.pallas_call(
+        functools.partial(whole_kernel, nlon, width, size),
+        out_shape=[
+            jax.ShapeDtypeStruct((3 * NUM, 2 * KMAX), jnp.float32),
+            jax.ShapeDtypeStruct((8, 128), jnp.float32),
+        ],
+        in_specs=[any_spec] * 5,
+        out_specs=[vmem, vmem],
+        scratch_shapes=[
+            pltpu.SMEM((GROUP,), jnp.int32),
+            pltpu.SMEM((NUM,), jnp.int32),
+            pltpu.VMEM((GROUP, 3, GROUP, nlon), jnp.float32),
+            pltpu.VMEM((GROUP, GROUP, GROUP, nlon), jnp.float32),
+            pltpu.VMEM(fwd.shape, jnp.bfloat16),
+            pltpu.VMEM((3, NUM, width), jnp.float32),
+            pltpu.VMEM((GROUP, NUM, width), jnp.float32),
+            pltpu.VMEM((NUM, 1, 6 * KMAX), jnp.float32),
+            pltpu.VMEM((GROUP, GROUP, GROUP, 1, 6 * KMAX), jnp.float32),
+            pltpu.VMEM((2, 128), jnp.float32),
+            pltpu.VMEM((GROUP, 2, 128), jnp.float32),
+            dma((5,)),
+        ] + [dma((GROUP,))] * 12,
+        compiler_params=pltpu.CompilerParams(
+            collective_id=0, has_side_effects=True, vmem_limit_bytes=24 << 20
+        ),
+        cost_estimate=pl.CostEstimate(flops=10**9, bytes_accessed=10**8, transcendentals=0),
+    )(*[pltpu.with_memory_space_constraint(a, pltpu.HBM) for a in (order, band_cut, vectors, flow, jnp.asarray(fwd))])
     return tuple(pl.pallas_call(
-        functools.partial(whole_kernel, nlon, width, size),
+        final_kernel,
         out_shape=[
             jax.ShapeDtypeStruct(vectors.shape, jnp.float32),
             jax.ShapeDtypeStruct((GROUP,), jnp.float32),
         ],
-        in_specs=[smem, smem, any_spec, any_spec, any_spec, any_spec],
-        out_specs=[pl.BlockSpec(memory_space=pltpu.VMEM), smem],
-        scratch_shapes=[
-            pltpu.VMEM((GROUP, 3, GROUP, nlon), jnp.float32),
-            pltpu.VMEM((GROUP, GROUP, GROUP, nlon), jnp.float32),
-            pltpu.VMEM(fwd.shape, jnp.bfloat16),
-            pltpu.VMEM(inv.shape, jnp.bfloat16),
-            pltpu.VMEM((3, NUM, width), jnp.float32),
-            pltpu.VMEM((GROUP, NUM, width), jnp.float32),
-            pltpu.VMEM((NUM, 1, 6 * KMAX), jnp.float32),
-            pltpu.VMEM((GROUP, NUM, 1, 6 * KMAX), jnp.float32),
-            pltpu.VMEM((2, 128), jnp.float32),
-            pltpu.VMEM((NUM, 2, 128), jnp.float32),
-            pltpu.VMEM((3 * NUM, 2 * KMAX), jnp.float32),
-            dma((4,)),
-            dma((GROUP,)), dma((GROUP,)), dma((GROUP,)), dma((GROUP,)), dma((GROUP,)), dma((GROUP,)),
-            dma((NUM,)), dma((NUM,)), dma((GROUP,)), dma((GROUP,)), dma((NUM,)), dma((NUM,)),
-        ],
-        compiler_params=pltpu.CompilerParams(
-            collective_id=0, has_side_effects=True, vmem_limit_bytes=40 << 20
-        ),
-    )(order, band_cut, vectors, flow, jnp.asarray(fwd), jnp.asarray(inv)))
+        in_specs=[vmem] * 3,
+        out_specs=[vmem, smem],
+        compiler_params=pltpu.CompilerParams(vmem_limit_bytes=24 << 20),
+    )(fresh, mix, jnp.asarray(inv)))
 
 
 def solution(mesh):

time: 41.6 us -> 35 us (0.84)
  local copies, waits for them, and re-layouts: 7.2 us -> 0.01 us
  Pallas kernels: 33.5 us -> 34.2 us
    unnamed x14 -> x2, local copies, waits for them, and re-layouts: 7.2 us -> 0.01 us
    pallas_call x0 -> x1, Pallas kernels: none -> 1.24 us  [on_group(): pl.pallas_call(final_kernel, out_shape=[jax.ShapeDtypeStruct(vectors.shap...]
    pallas_call x1, Pallas kernels: 33.5 us -> 32.9 us  [on_group(): pl.pallas_call(functools.partial(whole_kernel, nlon, width, size), out_sh...]
where the time goes in v2:
time: 35 us; the launch traced here: 34.8 us
  Pallas kernels  34.2 us (98%)
  between operations  0.65 us (2%)
    pallas_call x1, Pallas kernels, on_group(): pl.pallas_call(functools.partial(whole_kernel, nlon, width, size), out_sh...  32.9 us
    pallas_call x1, Pallas kernels, on_group(): pl.pallas_call(final_kernel, out_shape=[jax.ShapeDtypeStruct(vectors.shap...  1.24 us

profile of v2, /device:TPU:0, one launch (start us, length us, event | category | flops | bytes accessed | tf_op | source)
XLA Modules:
  0.0 34.8 jit_solution(995309867300369885)
XLA Ops:
  0.6 0.0 copy-start
  0.6 32.9 %shard_map.77 = (f32[48,256]{1,0:T(8,128)S(1)}, f32[8,128]{1,0:T(8,128)S(1)}) custom-call(s32[4]{0:T(128)} %order_hbm.1, s32[16]{0:T(128)} %cut_hbm.1, f32[4,3,4,1440]{3,2,1,0:T(4,128)} %vec_hbm.1, f32[4,4,1440]{2,1,0:T(4,128)} %flow_hbm.1, bf16[2,1536,256]{2,1,0:T(8,128)(2,1)} %constant.4.clone.fwd_hbm), custom_call_target="tpu_custom_call" | custom-call | flops 1000000000 | bytes 100000000 | tf_op jit(solution)/shard_map/pallas_call | solution.py:393
  33.6 0.0 copy-done
  33.6 1.2 %shard_map.78 = (f32[4,3,4,1440]{3,2,1,0:T(4,128)}, f32[4]{0:T(128)}) custom-call(f32[48,256]{1,0:T(8,128)S(1)} %get-tuple-element.4.nb, f32[8,128]{1,0:T(8,128)S(1)} %get-tuple-element.5.mix_ref, bf16[2,256,1440]{2,1,0:T(8,128)(2,1)S(1)} %copy-done), custom_call_target="tpu_custom_call" | custom-call | tf_op jit(solution)/shard_map/pallas_call | solution.py:420
Async XLA Ops:
  0.6 33.0 %copy-start = (bf16[2,256,1440]{2,1,0:T(8,128)(2,1)S(1)}, bf16[2,256,1440]{2,1,0:T(8,128)(2,1)}, u32[]{:S(2)}) copy-start(bf16[2,256,1440]{2,1,0:T(8,128)(2,1)} %constant.5.clone.inv_ref) | copy-start | bytes 4423684

commit v3 on v2

--- a/solution.py
+++ b/solution.py
@@ -305,45 +305,42 @@
         kept = jnp.where(keep, modes[NUM * f : NUM * (f + 1)], 0.0)
         sbuf[:, 0, 2 * KMAX * f : 2 * KMAX * (f + 1)] = kept
 
+    me = GROUP * v + b
+    peers = [(bands[j], vecs[k]) for j in (2, 3, 1, 0) for k in (2, 3, 1, 0)][:-1]
     mode_copies = []
-    for k in range(1, GROUP):
-        b2 = bands[k]
-        rows = pl.ds(pl.multiple_of(GROUP * b2, GROUP), GROUP)
-        mode_copies.append(remote(sbuf.at[rows], cs.at[v, b], csend.at[k], crecv.at[k], b2, v))
+    for k, (b2, v2) in enumerate(peers):
+        mode_copies.append(
+            remote(sbuf.at[GROUP * b2 + v2], cs.at[v2, me], csend.at[k], crecv.at[k], b2, v2)
+        )
         mode_copies[-1].start()
-    cs[v, b] = sbuf[pl.ds(pl.multiple_of(GROUP * b, GROUP), GROUP)]
+    cs[v, me] = sbuf[GROUP * b + v]
     for copy in mode_copies:
         copy.wait_recv()
+
+    part = cs[v].reshape(NUM, 6 * KMAX)
+    tiled = jnp.concatenate([part] * 8, axis=0)
+    product = lax.dot_general(
+        part, tiled, (((1,), (1,)), ((), ())), precision=HIGHEST,
+        preferred_element_type=jnp.float32,
+    )
+    product = jnp.where(diagonal, product, 0.0)
+    gsend[0:1, :] = jnp.sum(product[:8], axis=0, keepdims=True)
+    gsend[1:2, :] = jnp.sum(product[8:], axis=0, keepdims=True)
+    gram_copies = []
+    for k, (b2, v2) in enumerate(peers):
+        gram_copies.append(remote(gsend, gbuf.at[me], msend.at[k], mrecv.at[k], b2, v2))
+        gram_copies[-1].start()
     gathers = []
     for k in range(1, GROUP):
         v2 = vecs[k]
         gathers.append(remote(cs.at[v], cs.at[v], asend.at[k], arecv.at[k], b, v2))
         gathers[-1].start()
-    for copy in gathers:
-        copy.wait_recv()
-
-    product = 0.0
-    parts = []
-    for r in range(GROUP):
-        part = cs[:, :, r].reshape(NUM, 6 * KMAX)
-        parts.append(part)
-        tiled = jnp.concatenate([part] * 8, axis=0)
-        product = product + lax.dot_general(
-            part, tiled, (((1,), (1,)), ((), ())), precision=HIGHEST,
-            preferred_element_type=jnp.float32,
-        )
-    product = jnp.where(diagonal, product, 0.0)
-    gsend[0:1, :] = jnp.sum(product[:8], axis=0, keepdims=True)
-    gsend[1:2, :] = jnp.sum(product[8:], axis=0, keepdims=True)
-    gram_copies = []
-    for k in range(1, GROUP):
-        b2 = bands[k]
-        gram_copies.append(remote(gsend, gbuf.at[b], msend.at[k], mrecv.at[k], b2, v))
-        gram_copies[-1].start()
-    gbuf[b] = gsend[...]
+    gbuf[me] = gsend[...]
     for copy in gram_copies:
         copy.wait_recv()
-    gram = (gbuf[0] + gbuf[1]) + (gbuf[2] + gbuf[3])
+    gram = gbuf[0]
+    for k in range(1, NUM):
+        gram = gram + gbuf[k]
     gram = gram * (1.0 / size)
     spread = jnp.concatenate(
         [jnp.broadcast_to(gram[i : i + 1], (8, 128)) for i in range(2)], axis=0
@@ -362,8 +359,10 @@
     mix = dot_full(own_rows[:, :NUM], mix)
     mix_ref[...] = mix
 
+    for copy in gathers:
+        copy.wait_recv()
     for r in range(GROUP):
-        fresh = dot_full(mix[:, :NUM], parts[r])
+        fresh = dot_full(mix[:, :NUM], cs[r].reshape(NUM, 6 * KMAX))
         for i in range(GROUP):
             for f in range(3):
                 at = 12 * i + GROUP * f + r
@@ -407,11 +406,11 @@
             pltpu.VMEM((3, NUM, width), jnp.float32),
             pltpu.VMEM((GROUP, NUM, width), jnp.float32),
             pltpu.VMEM((NUM, 1, 6 * KMAX), jnp.float32),
-            pltpu.VMEM((GROUP, GROUP, GROUP, 1, 6 * KMAX), jnp.float32),
+            pltpu.VMEM((GROUP, NUM, 1, 6 * KMAX), jnp.float32),
             pltpu.VMEM((2, 128), jnp.float32),
-            pltpu.VMEM((GROUP, 2, 128), jnp.float32),
+            pltpu.VMEM((NUM, 2, 128), jnp.float32),
             dma((5,)),
-        ] + [dma((GROUP,))] * 12,
+        ] + [dma((GROUP,))] * 6 + [dma((NUM,))] * 2 + [dma((GROUP,))] * 2 + [dma((NUM,))] * 2,
         compiler_params=pltpu.CompilerParams(
             collective_id=0, has_side_effects=True, vmem_limit_bytes=24 << 20
         ),

time: 35 us -> 32.8 us (0.937)
  Pallas kernels: 34.2 us -> 32 us
    pallas_call x1, Pallas kernels: 32.9 us -> 30.7 us  [on_group(): pl.pallas_call(functools.partial(whole_kernel, nlon, width, size), out_sh...]
where the time goes in v3:
time: 32.8 us; the launch traced here: 32.6 us
  Pallas kernels  32 us (98%)
  between operations  0.65 us (2%)
    pallas_call x1, Pallas kernels, on_group(): pl.pallas_call(functools.partial(whole_kernel, nlon, width, size), out_sh...  30.7 us
    pallas_call x1, Pallas kernels, on_group(): pl.pallas_call(final_kernel, out_shape=[jax.ShapeDtypeStruct(vectors.shap...  1.24 us

profile of v3, /device:TPU:0, one launch (start us, length us, event | category | flops | bytes accessed | tf_op | source)
XLA Modules:
  0.0 32.6 jit_solution(16854547807543651563)
XLA Ops:
  0.6 0.0 copy-start
  0.6 30.7 %shard_map.77 = (f32[48,256]{1,0:T(8,128)S(1)}, f32[8,128]{1,0:T(8,128)S(1)}) custom-call(s32[4]{0:T(128)} %order_hbm.1, s32[16]{0:T(128)} %cut_hbm.1, f32[4,3,4,1440]{3,2,1,0:T(4,128)} %vec_hbm.1, f32[4,4,1440]{2,1,0:T(4,128)} %flow_hbm.1, bf16[2,1536,256]{2,1,0:T(8,128)(2,1)} %constant.4.clone.fwd_hbm), custom_call_target="tpu_custom_call" | custom-call | flops 1000000000 | bytes 100000000 | tf_op jit(solution)/shard_map/pallas_call | solution.py:392
  31.4 0.0 copy-done
  31.4 1.2 %shard_map.78 = (f32[4,3,4,1440]{3,2,1,0:T(4,128)}, f32[4]{0:T(128)}) custom-call(f32[48,256]{1,0:T(8,128)S(1)} %get-tuple-element.4.nb, f32[8,128]{1,0:T(8,128)S(1)} %get-tuple-element.5.mix_ref, bf16[2,256,1440]{2,1,0:T(8,128)(2,1)S(1)} %copy-done), custom_call_target="tpu_custom_call" | custom-call | tf_op jit(solution)/shard_map/pallas_call | solution.py:419
Async XLA Ops:
  0.6 30.8 %copy-start = (bf16[2,256,1440]{2,1,0:T(8,128)(2,1)S(1)}, bf16[2,256,1440]{2,1,0:T(8,128)(2,1)}, u32[]{:S(2)}) copy-start(bf16[2,256,1440]{2,1,0:T(8,128)(2,1)} %constant.5.clone.inv_ref) | copy-start | bytes 4423684

commit v4 on v3

--- a/solution.py
+++ b/solution.py
@@ -152,7 +152,9 @@
 def dot_split(value, table_ref):
     high, low = halves(value)
     dot = functools.partial(jnp.dot, preferred_element_type=jnp.float32)
-    return dot(high, table_ref[0]) + (dot(low, table_ref[0]) + dot(high, table_ref[1]))
+    rows = value.shape[0]
+    both = dot(jnp.concatenate([high, low], axis=0), table_ref[0])
+    return both[:rows] + (both[rows:] + dot(high, table_ref[1]))
 
 
 def dot_full(left, right):
@@ -238,6 +240,17 @@
         vec_copies.append(remote(vec_hbm.at[b2], vbuf.at[b], vsend.at[k], vrecv.at[k], b2, v))
         vec_copies[-1].start()
 
+    forwards = []
+
+    def forward(j, piece, source):
+        for k in (2, 3, 1):
+            at = GROUP * j + k
+            forwards.append(
+                remote(piece, fbuf.at[v, source], gosend.at[at], gorecv.at[at], b, vecs[k])
+            )
+            forwards[-1].start()
+
+    forward(0, flow_hbm.at[v], b)
     own[3].wait()
     own[4].wait()
     lane = iota((NUM, 128), 1)
@@ -268,13 +281,10 @@
     keep = wave <= cut
 
     own[0].wait()
-    for copy in flow_copies:
-        copy.wait_recv()
-    forwards = []
-    for k in range(1, GROUP):
-        v2 = vecs[k]
-        forwards.append(remote(fbuf.at[v], fbuf.at[v], gosend.at[k], gorecv.at[k], b, v2))
-        forwards[-1].start()
+    for j in (1, 3, 2):
+        flow_copies[j - 1].wait_recv()
+        source = bands[GROUP - j]
+        forward(j, fbuf.at[v, source], source)
 
     own[1].wait()
     for copy in vec_copies:
@@ -410,7 +420,7 @@
             pltpu.VMEM((2, 128), jnp.float32),
             pltpu.VMEM((NUM, 2, 128), jnp.float32),
             dma((5,)),
-        ] + [dma((GROUP,))] * 6 + [dma((NUM,))] * 2 + [dma((GROUP,))] * 2 + [dma((NUM,))] * 2,
+        ] + [dma((GROUP,))] * 4 + [dma((NUM,))] * 4 + [dma((GROUP,))] * 2 + [dma((NUM,))] * 2,
         compiler_params=pltpu.CompilerParams(
             collective_id=0, has_side_effects=True, vmem_limit_bytes=24 << 20
         ),

time: 32.8 us -> 31.6 us (0.963)
  Pallas kernels: 32 us -> 30.8 us
    pallas_call x1, Pallas kernels: 30.7 us -> 29.7 us  [on_group(): pl.pallas_call(functools.partial(whole_kernel, nlon, width, size), out_sh...]
where the time goes in v4:
time: 31.6 us; the launch traced here: 31.5 us
  Pallas kernels  30.8 us (97%)
  between operations  0.65 us (2%)
    pallas_call x1, Pallas kernels, on_group(): pl.pallas_call(functools.partial(whole_kernel, nlon, width, size), out_sh...  29.7 us
    pallas_call x1, Pallas kernels, on_group(): pl.pallas_call(final_kernel, out_shape=[jax.ShapeDtypeStruct(vectors.shap...  1.09 us

profile of v4, /device:TPU:0, one launch (start us, length us, event | category | flops | bytes accessed | tf_op | source)
XLA Modules:
  0.0 31.5 jit_solution(4049358265922906390)
XLA Ops:
  0.6 0.0 copy-start
  0.6 29.7 %shard_map.77 = (f32[48,256]{1,0:T(8,128)S(1)}, f32[8,128]{1,0:T(8,128)S(1)}) custom-call(s32[4]{0:T(128)} %order_hbm.1, s32[16]{0:T(128)} %cut_hbm.1, f32[4,3,4,1440]{3,2,1,0:T(4,128)} %vec_hbm.1, f32[4,4,1440]{2,1,0:T(4,128)} %flow_hbm.1, bf16[2,1536,256]{2,1,0:T(8,128)(2,1)} %constant.4.clone.fwd_hbm), custom_call_target="tpu_custom_call" | custom-call | flops 1000000000 | bytes 100000000 | tf_op jit(solution)/shard_map/pallas_call | solution.py:402
  30.4 0.0 copy-done
  30.4 1.1 %shard_map.78 = (f32[4,3,4,1440]{3,2,1,0:T(4,128)}, f32[4]{0:T(128)}) custom-call(f32[48,256]{1,0:T(8,128)S(1)} %get-tuple-element.4.nb, f32[8,128]{1,0:T(8,128)S(1)} %get-tuple-element.5.mix_ref, bf16[2,256,1440]{2,1,0:T(8,128)(2,1)S(1)} %copy-done), custom_call_target="tpu_custom_call" | custom-call | tf_op jit(solution)/shard_map/pallas_call | solution.py:429
Async XLA Ops:
  0.6 29.7 %copy-start = (bf16[2,256,1440]{2,1,0:T(8,128)(2,1)S(1)}, bf16[2,256,1440]{2,1,0:T(8,128)(2,1)}, u32[]{:S(2)}) copy-start(bf16[2,256,1440]{2,1,0:T(8,128)(2,1)} %constant.5.clone.inv_ref) | copy-start | bytes 4423684

commit v5 on v4

--- a/solution.py
+++ b/solution.py
@@ -235,11 +235,6 @@
             remote(flow_hbm.at[v], fbuf.at[v, b], fsend.at[k], frecv.at[k], b2, v)
         )
         flow_copies[-1].start()
-    for k in range(1, GROUP):
-        b2 = bands[k]
-        vec_copies.append(remote(vec_hbm.at[b2], vbuf.at[b], vsend.at[k], vrecv.at[k], b2, v))
-        vec_copies[-1].start()
-
     forwards = []
 
     def forward(j, piece, source):
@@ -251,6 +246,12 @@
             forwards[-1].start()
 
     forward(0, flow_hbm.at[v], b)
+
+    for k in range(1, GROUP):
+        b2 = bands[k]
+        vec_copies.append(remote(vec_hbm.at[b2], vbuf.at[b], vsend.at[k], vrecv.at[k], b2, v))
+        vec_copies[-1].start()
+
     own[3].wait()
     own[4].wait()
     lane = iota((NUM, 128), 1)

time: 31.6 us -> 31.6 us (level)
  no operation moved by 1% of the time
where the time goes in v5:
time: 31.6 us; the launch traced here: 31.5 us
  Pallas kernels  30.8 us (97%)
  between operations  0.65 us (2%)
    pallas_call x1, Pallas kernels, on_group(): pl.pallas_call(functools.partial(whole_kernel, nlon, width, size), out_sh...  29.7 us
    pallas_call x1, Pallas kernels, on_group(): pl.pallas_call(final_kernel, out_shape=[jax.ShapeDtypeStruct(vectors.shap...  1.09 us

profile of v5, /device:TPU:0, one launch (start us, length us, event | category | flops | bytes accessed | tf_op | source)
XLA Modules:
  0.0 31.5 jit_solution(2482258521365727952)
XLA Ops:
  0.6 0.0 copy-start
  0.6 29.7 %shard_map.77 = (f32[48,256]{1,0:T(8,128)S(1)}, f32[8,128]{1,0:T(8,128)S(1)}) custom-call(s32[4]{0:T(128)} %order_hbm.1, s32[16]{0:T(128)} %cut_hbm.1, f32[4,3,4,1440]{3,2,1,0:T(4,128)} %vec_hbm.1, f32[4,4,1440]{2,1,0:T(4,128)} %flow_hbm.1, bf16[2,1536,256]{2,1,0:T(8,128)(2,1)} %constant.4.clone.fwd_hbm), custom_call_target="tpu_custom_call" | custom-call | flops 1000000000 | bytes 100000000 | tf_op jit(solution)/shard_map/pallas_call | solution.py:403
  30.4 0.0 copy-done
  30.4 1.1 %shard_map.78 = (f32[4,3,4,1440]{3,2,1,0:T(4,128)}, f32[4]{0:T(128)}) custom-call(f32[48,256]{1,0:T(8,128)S(1)} %get-tuple-element.4.nb, f32[8,128]{1,0:T(8,128)S(1)} %get-tuple-element.5.mix_ref, bf16[2,256,1440]{2,1,0:T(8,128)(2,1)S(1)} %copy-done), custom_call_target="tpu_custom_call" | custom-call | tf_op jit(solution)/shard_map/pallas_call | solution.py:430
Async XLA Ops:
  0.6 29.7 %copy-start = (bf16[2,256,1440]{2,1,0:T(8,128)(2,1)S(1)}, bf16[2,256,1440]{2,1,0:T(8,128)(2,1)}, u32[]{:S(2)}) copy-start(bf16[2,256,1440]{2,1,0:T(8,128)(2,1)} %constant.5.clone.inv_ref) | copy-start | bytes 4423684
